TPU v7x, 32 devices: a whole 2x2x4 slice. The times are simulated.
32 devices in a mesh: row: 4 (over z), col: 8 (over y, x, core).
Axes of the slice: x: 2, y: 2, z: 4, core: 2. Of those that a mesh axis runs over, the one named last changes fastest.
Arguments:
- amplitudes: bfloat16 [16, 16, 12, 4096], P('row', 'col'), may hold values from -6 to 6
- integrals: bfloat16 [16, 16, 47, 4096], P('row', 'col'), may hold values from -0.1875 to 0.1875
- pair_lists: int32 [4, 12, 2], replicated, may hold values from 0 to 46, as said below
- tile_counts: int32 [4], replicated, may hold values from 1 to 12, as said below
Outputs:
- symmetric: float32 [16, 16, 12, 4096], P('row', 'col')
Inputs may be any that keep to these rules, and one draw needn't show every extreme that they name: `pair_lists`: each grid row lists 12 distinct ordered pairs of different tiles. `tile_counts`: the largest count equals 12.
All inputs are finite; a program needn't handle non-finite values.
Results may differ from a plain program's by a relative error of at most 0.0029.
Values may be sent and summed in bfloat16 or wider, within the bound.
No kernel may reach another device: no remote copies, remote signals or barrier semaphores. Data moves between devices by JAX's collectives and lax.ppermute only.
A program may use at most 128 MiB of HBM per device.

v0:
```python
import jax
import jax.numpy as jnp
from jax import lax
from jax.sharding import PartitionSpec as P

TILE = 64


def on_device(amplitudes, integrals, pair_lists, tile_counts):
    occ_row, occ_col, slot_count, square = amplitudes.shape
    tile_width = TILE
    row_devices = lax.axis_size("row")
    col_devices = lax.axis_size("col")
    col_ratio = col_devices // row_devices
    my_row = lax.axis_index("row")
    my_col = lax.axis_index("col")
    partner_row = my_col // col_ratio
    tile_first = pair_lists[:, :, 0]
    tile_second = pair_lists[:, :, 1]
    packed = jnp.take(integrals, tile_second.reshape(-1), axis=2)
    packed = packed.reshape(occ_row, occ_col, row_devices, slot_count, square)
    received = lax.all_to_all(packed, "row", split_axis=2, concat_axis=0, tiled=True)
    received = received.reshape(occ_row * row_devices, occ_col, slot_count, square)
    piece = lax.all_gather(amplitudes, "col", axis=1, tiled=True)
    piece_count = piece.shape[1]
    left_tiles = piece.reshape(occ_row, piece_count, slot_count, tile_width, tile_width)
    right_tiles = received.reshape(piece_count, occ_col, slot_count, tile_width, tile_width)
    cycle_sum = jnp.einsum(
        "iksac,kjscb->ijsab", left_tiles, right_tiles, preferred_element_type=jnp.float32
    )
    my_count = lax.dynamic_index_in_dim(tile_counts, my_row, 0, keepdims=False)
    live_slots = (jnp.arange(slot_count, dtype=jnp.int32) < my_count).astype(jnp.float32)
    cycle_value = (cycle_sum * live_slots[None, None, :, None, None]).astype(jnp.bfloat16)
    cycle = cycle_value.reshape(occ_row, occ_col, slot_count, square)
    residual_strip = lax.all_gather(cycle, "row", axis=0, tiled=True)
    mirror_whole = lax.all_to_all(residual_strip, "col", split_axis=0, concat_axis=1, tiled=True)
    mirror_block = lax.dynamic_slice_in_dim(mirror_whole, my_row * occ_row, occ_row, 1)
    mirror_block = mirror_block.reshape(occ_col, occ_row, slot_count, tile_width, tile_width)
    mine_first = lax.dynamic_index_in_dim(tile_first, my_row, 0, keepdims=False)
    mine_second = lax.dynamic_index_in_dim(tile_second, my_row, 0, keepdims=False)
    their_first = lax.dynamic_index_in_dim(tile_first, partner_row, 0, keepdims=False)
    their_second = lax.dynamic_index_in_dim(tile_second, partner_row, 0, keepdims=False)
    pair_match = (
        (mine_first[:, None] == their_second[None, :])
        & (mine_second[:, None] == their_first[None, :])
    ).astype(jnp.bfloat16)
    crossed = jnp.einsum(
        "st,jitba->ijsab", pair_match, mirror_block, preferred_element_type=jnp.float32
    )
    own_part = cycle_value.astype(jnp.float32)
    symmetric = (own_part + crossed) * live_slots[None, None, :, None, None]
    return symmetric.reshape(occ_row, occ_col, slot_count, square)


def solution(mesh):
    return jax.shard_map(
        on_device,
        mesh=mesh,
        in_specs=(P("row", "col", None, None), P("row", "col", None, None), P(), P()),
        out_specs=P("row", "col", None, None),
        check_vma=False,
    )
```

profile of v0, /device:TPU:0, one launch (start us, length us, event | category | flops | bytes accessed | tf_op | source)
XLA Modules:
  0.0 288.4 jit_solution(7167490492308642510)
XLA Ops:
  6.5 0.0 copy-start
  6.5 0.0 all-gather.3.cloned.1.call-start
  6.5 2.8 copy.17
  9.3 0.0 all-gather.3.cloned.1.call-update
  9.3 0.8 fusion.29
  10.1 0.1 reshape_squeeze.6
  10.2 8.5 %gather_fusion = bf16[48,4,2,4096]{3,2,1,0:T(2,128)(2,1)} fusion(bf16[4,2,47,4096]{3,1,2,0:T(2,128)(2,1)S(1)} %copy-done, s32[1024]{0:T(1024)S(1)} %pad_clamp_fusion), kind=kCustom, calls=%fused_computation | custom fusion | bytes 6291648 | tf_op jit(solution)/shard_map/jit(_take)/gather | solution.py:20
  18.8 6.7 %broadcast_select_fusion = bf16[4,2,4,12,4096]{4,1,3,0,2:T(2,128)(2,1)} fusion(pred[4,12]{1,0:T(4,128)(4,1)S(1)} %compare_and_fusion, bf16[4,2,4,12,4096]{4,1,0,3,2:T(2,128)(2,1)} %bitcast.67), kind=kLoop, calls=%fused_computation.4 | loop fusion | flops 1572864 | bytes 6291504 | tf_op jit(solution)/shard_map/jit(_take)/select_n | solution.py:20
  25.4 6.4 %all-to-all-start = ((bf16[4,2,4,12,4096]{4,1,3,0,2:T(2,128)(2,1)}), bf16[4,2,4,12,4096]{4,1,3,0,2:T(2,128)(2,1)}, u32[]{:S(2)}, u32[]{:S(2)}) async-start(bf16[4,2,4,12,4096]{4,1,3,0,2:T(2,128)(2,1)} %broadcast_select_fusion), calls=%async_computation | async-start | bytes 6291456 | tf_op jit(solution)/shard_map/all_to_all | solution.py:22
  31.9 0.0 all-gather.5.cloned.1.call-start
  31.9 0.6 dynamic_slice.20
  32.5 0.6 compare_convert_fusion
  33.1 69.6 %all-to-all-done = bf16[4,2,4,12,4096]{4,1,3,0,2:T(2,128)(2,1)} async-done(((bf16[4,2,4,12,4096]{4,1,3,0,2:T(2,128)(2,1)}), bf16[4,2,4,12,4096]{4,1,3,0,2:T(2,128)(2,1)}, u32[]{:S(2)}, u32[]{:S(2)}) %all-to-all-start) | async-done | bytes 3145760 | tf_op jit(solution)/shard_map/all_to_all | solution.py:22
  102.7 11.1 %reshape_reshape.3 = bf16[16,2,12,64,64]{4,3,1,2,0:T(8,128)(2,1)} reshape(bf16[4,4,2,1,12,4096]{5,2,4,1,0,3:T(2,128)(2,1)} %bitcast.5) | data formatting | bytes 6291456 | tf_op jit(solution)/shard_map/reshape;reshape | solution.py:27
  113.8 9.4 %copy.18 = bf16[4,16,12,4096]{3,1,0,2:T(8,128)(2,1)} copy(bf16[4,16,12,4096]{3,0,2,1:T(4,128)(2,1)} %all-gather.3.cloned.1.call-done) | data formatting | bytes 12582912 | tf_op jit(solution)/shard_map/all_gather | solution.py:24
  123.2 17.9 %reshape.81 = bf16[4,16,12,64,64,1]{4,3,1,0,2,5:T(8,128)(2,1)} reshape(bf16[4,16,12,4096]{3,1,0,2:T(8,128)(2,1)} %copy.18) | data formatting | bytes 12582912 | tf_op jit(solution)/shard_map/reshape | solution.py:26
  141.1 11.1 %fusion.11 = bf16[4,2,12,64,64]{3,4,0,1,2:T(8,128)(2,1)S(1)} fusion(f32[12]{0:T(128)S(1)} %compare_convert_fusion, bf16[4,16,12,64,64,1]{4,3,1,0,2,5:T(8,128)(2,1)} %reshape.81, bf16[16,2,12,64,64]{4,3,1,2,0:T(8,128)(2,1)} %reshape_reshape.3), kind=kOutput, calls=%fused_computation.11 | convolution fusion | flops 806092800 | bytes 10223664 | tf_op jit(solution)/shard_map/iksac,kjscb->ijsab/dot_general | solution.py:28
  152.2 1.7 copy.20
  153.9 3.9 %reshape.69 = bf16[4,2,12,4096]{3,1,2,0:T(2,128)(2,1)} reshape(bf16[4,2,12,64,64]{4,3,1,2,0:T(8,128)(2,1)} %copy.20) | data formatting | bytes 1572864 | tf_op jit(solution)/shard_map/reshape | solution.py:34
  157.7 0.0 all-gather.5.cloned.1.call-update
  157.8 0.0 copy-done.2
  157.8 62.7 %all-gather.5.cloned.1.call-done = bf16[16,2,12,4096]{3,1,2,0:T(2,128)(2,1)} async-done(((bf16[4,2,12,4096]{3,1,2,0:T(2,128)(2,1)}), bf16[16,2,12,4096]{3,1,2,0:T(2,128)(2,1)}) %all-gather.5.cloned.1.call-update) | async-done | bytes 3145744 | tf_op jit(solution)/shard_map/all_gather | solution.py:35
  220.4 4.7 %all-to-all-start.1 = ((bf16[16,2,12,4096]{3,1,2,0:T(2,128)(2,1)}), bf16[16,2,12,4096]{3,1,2,0:T(2,128)(2,1)}, u32[]{:S(2)}, u32[]{:S(2)}) async-start(bf16[16,2,12,4096]{3,1,2,0:T(2,128)(2,1)} %all-gather.5.cloned.1.call-done), calls=%async_computation.1 | async-start | bytes 6291456 | tf_op jit(solution)/shard_map/all_to_all | solution.py:36
  225.2 37.6 %all-to-all-done.1 = bf16[16,2,12,4096]{3,1,2,0:T(2,128)(2,1)} async-done(((bf16[16,2,12,4096]{3,1,2,0:T(2,128)(2,1)}), bf16[16,2,12,4096]{3,1,2,0:T(2,128)(2,1)}, u32[]{:S(2)}, u32[]{:S(2)}) %all-to-all-start.1) | async-done | bytes 3145760 | tf_op jit(solution)/shard_map/all_to_all | solution.py:36
  262.8 5.1 %copy.21 = bf16[8,2,2,12,4096]{4,1,3,2,0:T(2,128)(2,1)S(1)} copy(bf16[8,2,2,12,4096]{4,2,3,1,0:T(2,128)(2,1)} %bitcast.12) | data formatting | bytes 6291456 | tf_op jit(solution)/shard_map/all_to_all | solution.py:36
  267.9 0.7 constant_dynamic-slice_fusion.4
  268.6 1.0 reshape.85
  269.6 1.1 fusion.5
  270.7 0.3 copy-done.3
  271.0 2.7 fusion.3
  273.7 3.7 %copy.25 = f32[4,2,12,64,64]{4,3,1,2,0:T(8,128)} copy(f32[4,2,12,64,64]{3,4,0,1,2:T(8,128)} %fusion.3) | data formatting | bytes 3145728 | tf_op jit(solution)/shard_map/mul | solution.py:51
  277.4 4.2 %reshape.71 = f32[4,2,12,4096]{3,1,2,0:T(2,128)} reshape(f32[4,2,12,64,64]{4,3,1,2,0:T(8,128)} %copy.25) | data formatting | bytes 3145728 | tf_op jit(solution)/shard_map/reshape | solution.py:52
  (12 shorter events, 0.0 us)
Async XLA Ops:
  6.5 3.7 %copy-start = (bf16[4,2,47,4096]{3,1,2,0:T(2,128)(2,1)S(1)}, bf16[4,2,47,4096]{3,1,2,0:T(2,128)(2,1)}, u32[]{:S(2)}) copy-start(bf16[4,2,47,4096]{3,1,2,0:T(2,128)(2,1)} %param.5) | copy-start | bytes 9240580
  6.5 107.3 %all-gather.3.cloned.1.call-start = ((), (), s32[]{:S(2)}) async-start(), calls=%async_computation.2 | async-start | bytes 7077888 | tf_op jit(solution)/shard_map/all_gather | solution.py:24
  25.4 6.4 %copy-start.4 = (s32[4]{0:T(128)S(1)}, s32[4]{0:T(128)}, u32[]{:S(2)}) copy-start(s32[4]{0:T(128)} %param.7) | copy-start | bytes 52
  25.4 77.3 %all-to-all-start = ((bf16[4,2,4,12,4096]{4,1,3,0,2:T(2,128)(2,1)}), bf16[4,2,4,12,4096]{4,1,3,0,2:T(2,128)(2,1)}, u32[]{:S(2)}, u32[]{:S(2)}) async-start(bf16[4,2,4,12,4096]{4,1,3,0,2:T(2,128)(2,1)} %broadcast_select_fusion), calls=%async_computation | async-start | bytes 6291456 | tf_op jit(solution)/shard_map/all_to_all | solution.py:22
  31.9 188.6 %all-gather.5.cloned.1.call-start = ((), (), s32[]{:S(2)}) async-start(), calls=%async_computation.3 | async-start | bytes 3932160 | tf_op jit(solution)/shard_map/all_gather | solution.py:35
  152.2 5.6 %copy-start.2 = (bf16[4,2,12,64,64]{3,4,0,1,2:T(8,128)(2,1)}, bf16[4,2,12,64,64]{3,4,0,1,2:T(8,128)(2,1)S(1)}, u32[]{:S(2)}) copy-start(bf16[4,2,12,64,64]{3,4,0,1,2:T(8,128)(2,1)S(1)} %fusion.11) | copy-start | bytes 2359300
  220.4 42.3 %all-to-all-start.1 = ((bf16[16,2,12,4096]{3,1,2,0:T(2,128)(2,1)}), bf16[16,2,12,4096]{3,1,2,0:T(2,128)(2,1)}, u32[]{:S(2)}, u32[]{:S(2)}) async-start(bf16[16,2,12,4096]{3,1,2,0:T(2,128)(2,1)} %all-gather.5.cloned.1.call-done), calls=%async_computation.1 | async-start | bytes 6291456 | tf_op jit(solution)/shard_map/all_to_all | solution.py:36
  269.6 1.4 copy-start.3
  273.7 7.9 %copy-start.1 = (bf16[4,2,47,4096]{3,1,2,0:T(2,128)(2,1)S(1)}, bf16[4,2,47,4096]{3,1,2,0:T(2,128)(2,1)}, u32[]{:S(2)}) copy-start(bf16[4,2,47,4096]{3,1,2,0:T(2,128)(2,1)} %param.5) | copy-start | bytes 9240580
Sparse Core Ops, SparseCore 0:
  9.5 48.1 all-gather.2
  157.9 62.5 all-gather.4
where the time goes:
time: 290 us; the launch traced here: 288 us
  waiting for transfers between devices  170 us (59%)
  local copies, waits for them, and re-layouts  71.7 us (25%)
  between operations  13.5 us (5%)
  matrix products  12.2 us (4%)
  starting transfers between devices  11.1 us (4%)
  other arithmetic  10 us (3%)
    all_to_all x1, waiting for transfers between devices, on_device(): lax.all_to_all(packed, 'row', split_axis=2, concat_axis=0, tiled=True)  69.6 us
    all_gather x1, waiting for transfers between devices, on_device(): residual_strip = lax.all_gather(cycle, 'row', axis=0, tiled=True)  62.7 us
    all_to_all x1, waiting for transfers between devices, on_device(): lax.all_to_all(residual_strip, 'col', split_axis=0, concat_axis=1, tiled=...  37.6 us
    reshape x1, local copies, waits for them, and re-layouts, on_device(): piece.reshape(occ_row, piece_count, slot_count, tile_width, tile_width)  17.9 us
    another operation x1, local copies, waits for them, and re-layouts, on_device(): received.reshape(piece_count, occ_col, slot_count, tile_width, tile_width)  11.1 us
    dot_general x1, matrix products, on_device(): jnp.einsum('iksac,kjscb->ijsab', left_tiles, right_tiles, preferred_eleme...  11.1 us
    all_gather x1, local copies, waits for them, and re-layouts, on_device(): piece = lax.all_gather(amplitudes, 'col', axis=1, tiled=True)  9.35 us
    gather x1, local copies, waits for them, and re-layouts, on_device(): packed = jnp.take(integrals, tile_second.reshape(-1), axis=2)  8.51 us
  transfers between devices with their start and end apart: 4, of which 3 were waited for; matrix products, arithmetic and copies ran while one was open for 10% of the time, Pallas kernels for 0%

commit v1 on v0

--- a/solution.py
+++ b/solution.py
@@ -32,7 +32,12 @@
     live_slots = (jnp.arange(slot_count, dtype=jnp.int32) < my_count).astype(jnp.float32)
     cycle_value = (cycle_sum * live_slots[None, None, :, None, None]).astype(jnp.bfloat16)
     cycle = cycle_value.reshape(occ_row, occ_col, slot_count, square)
-    residual_strip = lax.all_gather(cycle, "row", axis=0, tiled=True)
+    ring = [cycle]
+    for hop in range(3):
+        ring.append(lax.ppermute(ring[-1], "row", [(dev, (dev + 1) % 4) for dev in range(4)]))
+    residual_strip = jnp.roll(
+        jnp.concatenate(ring[::-1], axis=0), (lax.axis_index("row") + 1) * ring[0].shape[0], axis=0
+    )
     mirror_whole = lax.all_to_all(residual_strip, "col", split_axis=0, concat_axis=1, tiled=True)
     mirror_block = lax.dynamic_slice_in_dim(mirror_whole, my_row * occ_row, occ_row, 1)
     mirror_block = mirror_block.reshape(occ_col, occ_row, slot_count, tile_width, tile_width)

time: 290 us -> 300 us (1.034)
  local copies, waits for them, and re-layouts: 71.7 us -> 86.3 us
  waiting for transfers between devices: 170 us -> 166 us
    all_gather x1 -> x0, waiting for transfers between devices: 62.7 us -> none  [on_device(): residual_strip = lax.all_gather(cycle, 'row', axis=0, tiled=True)]
    ppermute x0 -> x3, waiting for transfers between devices: none -> 58.3 us  [on_device(): lax.ppermute(ring[-1], 'row', [(dev, (dev + 1) % 4) for dev in range(4)])]
    unnamed x11 -> x18, local copies, waits for them, and re-layouts: 3.1 us -> 13 us
    dynamic_slice x0 -> x1, local copies, waits for them, and re-layouts: none -> 4.73 us  [on_device(): jnp.roll(jnp.concatenate(ring[::-1], axis=0), (lax.axis_index('row') + 1)...]
  transfers between devices with their start and end apart: 4 -> 6, of which waited for: 3 -> 5; matrix products, arithmetic and copies ran while one was open for 10% -> 10% of each run, Pallas kernels for 0% -> 0%
where the time goes in v1:
time: 300 us; the launch traced here: 299 us
  waiting for transfers between devices  166 us (55%)
  local copies, waits for them, and re-layouts  86.3 us (29%)
  between operations  13.6 us (5%)
  matrix products  12.2 us (4%)
  starting transfers between devices  11.2 us (4%)
  other arithmetic  10 us (3%)
    all_to_all x1, waiting for transfers between devices, on_device(): lax.all_to_all(packed, 'row', split_axis=2, concat_axis=0, tiled=True)  69.8 us
    ppermute x3, waiting for transfers between devices, on_device(): lax.ppermute(ring[-1], 'row', [(dev, (dev + 1) % 4) for dev in range(4)])  58.3 us
    all_to_all x1, waiting for transfers between devices, on_device(): lax.all_to_all(residual_strip, 'col', split_axis=0, concat_axis=1, tiled=...  37.6 us
    reshape x1, local copies, waits for them, and re-layouts, on_device(): piece.reshape(occ_row, piece_count, slot_count, tile_width, tile_width)  17.9 us
    unnamed x18, local copies, waits for them, and re-layouts  13 us
    another operation x1, local copies, waits for them, and re-layouts, on_device(): received.reshape(piece_count, occ_col, slot_count, tile_width, tile_width)  11.1 us
    dot_general x1, matrix products, on_device(): jnp.einsum('iksac,kjscb->ijsab', left_tiles, right_tiles, preferred_eleme...  11.1 us
    all_gather x1, local copies, waits for them, and re-layouts, on_device(): piece = lax.all_gather(amplitudes, 'col', axis=1, tiled=True)  9.35 us
  transfers between devices with their start and end apart: 6, of which 5 were waited for; matrix products, arithmetic and copies ran while one was open for 10% of the time, Pallas kernels for 0%

profile of v1, /device:TPU:0, one launch (start us, length us, event | category | flops | bytes accessed | tf_op | source)
XLA Modules:
  0.0 298.9 jit_solution(12801907893527067175)
XLA Ops:
  6.5 2.8 copy.17
  10.2 8.5 %gather_fusion = bf16[48,4,2,4096]{3,2,1,0:T(2,128)(2,1)} fusion(bf16[4,2,47,4096]{3,1,2,0:T(2,128)(2,1)S(1)} %copy-done, s32[1024]{0:T(1024)S(1)} %pad_clamp_fusion), kind=kCustom, calls=%fused_computation | custom fusion | bytes 6291648 | tf_op jit(solution)/shard_map/jit(_take)/gather | solution.py:20
  18.8 6.7 %broadcast_select_fusion = bf16[4,2,4,12,4096]{4,1,3,0,2:T(2,128)(2,1)} fusion(pred[4,12]{1,0:T(4,128)(4,1)S(1)} %compare_and_fusion, bf16[4,2,4,12,4096]{4,1,0,3,2:T(2,128)(2,1)} %bitcast.67), kind=kLoop, calls=%fused_computation.4 | loop fusion | flops 1572864 | bytes 6291504 | tf_op jit(solution)/shard_map/jit(_take)/select_n | solution.py:20
  25.4 6.4 %all-to-all-start = ((bf16[4,2,4,12,4096]{4,1,3,0,2:T(2,128)(2,1)}), bf16[4,2,4,12,4096]{4,1,3,0,2:T(2,128)(2,1)}, u32[]{:S(2)}, u32[]{:S(2)}) async-start(bf16[4,2,4,12,4096]{4,1,3,0,2:T(2,128)(2,1)} %broadcast_select_fusion), calls=%async_computation | async-start | bytes 6291456 | tf_op jit(solution)/shard_map/all_to_all | solution.py:22
  33.1 69.8 %all-to-all-done = bf16[4,2,4,12,4096]{4,1,3,0,2:T(2,128)(2,1)} async-done(((bf16[4,2,4,12,4096]{4,1,3,0,2:T(2,128)(2,1)}), bf16[4,2,4,12,4096]{4,1,3,0,2:T(2,128)(2,1)}, u32[]{:S(2)}, u32[]{:S(2)}) %all-to-all-start) | async-done | bytes 3145760 | tf_op jit(solution)/shard_map/all_to_all | solution.py:22
  102.9 11.1 %reshape_reshape.3 = bf16[16,2,12,64,64]{4,3,1,2,0:T(8,128)(2,1)} reshape(bf16[4,4,2,1,12,4096]{5,2,4,1,0,3:T(2,128)(2,1)} %bitcast.5) | data formatting | bytes 6291456 | tf_op jit(solution)/shard_map/reshape;reshape | solution.py:27
  114.0 9.4 %copy.18 = bf16[4,16,12,4096]{3,1,0,2:T(8,128)(2,1)} copy(bf16[4,16,12,4096]{3,0,2,1:T(4,128)(2,1)} %all-gather.2.cloned.1.call-done) | data formatting | bytes 12582912 | tf_op jit(solution)/shard_map/all_gather | solution.py:24
  123.4 17.9 %reshape.81 = bf16[4,16,12,64,64,1]{4,3,1,0,2,5:T(8,128)(2,1)} reshape(bf16[4,16,12,4096]{3,1,0,2:T(8,128)(2,1)} %copy.18) | data formatting | bytes 12582912 | tf_op jit(solution)/shard_map/reshape | solution.py:26
  141.3 11.1 %fusion.11 = bf16[4,2,12,64,64]{3,4,0,1,2:T(8,128)(2,1)S(1)} fusion(f32[12]{0:T(128)S(1)} %compare_convert_fusion, bf16[4,16,12,64,64,1]{4,3,1,0,2,5:T(8,128)(2,1)} %reshape.81, bf16[16,2,12,64,64]{4,3,1,2,0:T(8,128)(2,1)} %reshape_reshape.3), kind=kOutput, calls=%fused_computation.11 | convolution fusion | flops 806092800 | bytes 10223664 | tf_op jit(solution)/shard_map/iksac,kjscb->ijsab/dot_general | solution.py:28
  152.4 1.1 copy-done.2
  153.5 1.6 copy.20
  155.1 3.1 %reshape.69 = bf16[4,2,12,4096]{3,1,2,0:T(2,128)(2,1)S(1)} reshape(bf16[4,2,12,64,64]{4,3,1,2,0:T(8,128)(2,1)} %copy.20) | data formatting | bytes 1572864 | tf_op jit(solution)/shard_map/reshape | solution.py:34
  158.3 20.2 %collective-permute-done = bf16[4,2,12,4096]{3,1,2,0:T(2,128)(2,1)S(1)} collective-permute-done((bf16[4,2,12,4096]{3,1,2,0:T(2,128)(2,1)S(1)}, bf16[4,2,12,4096]{3,1,2,0:T(2,128)(2,1)S(1)}, u32[]{:S(2)}, u32[]{:S(2)}) %collective-permute-start) | collective-permute-done | bytes 786464 | tf_op jit(solution)/shard_map/ppermute | solution.py:37
  178.5 19.4 %collective-permute-done.1 = bf16[4,2,12,4096]{3,1,2,0:T(2,128)(2,1)S(1)} collective-permute-done((bf16[4,2,12,4096]{3,1,2,0:T(2,128)(2,1)S(1)}, bf16[4,2,12,4096]{3,1,2,0:T(2,128)(2,1)S(1)}, u32[]{:S(2)}, u32[]{:S(2)}) %collective-permute-start.1) | collective-permute-done | bytes 786464 | tf_op jit(solution)/shard_map/ppermute | solution.py:37
  197.9 18.6 %collective-permute-done.2 = bf16[4,2,12,4096]{3,1,2,0:T(2,128)(2,1)} collective-permute-done((bf16[4,2,12,4096]{3,1,2,0:T(2,128)(2,1)S(1)}, bf16[4,2,12,4096]{3,1,2,0:T(2,128)(2,1)}, u32[]{:S(2)}, u32[]{:S(2)}) %collective-permute-start.2) | collective-permute-done | bytes 786464 | tf_op jit(solution)/shard_map/ppermute | solution.py:37
  216.5 1.8 constant_dynamic-update-slice_fusion.7
  218.3 1.0 constant_dynamic-update-slice_fusion.6
  219.3 1.0 constant_dynamic-update-slice_fusion.5
  220.3 1.0 constant_dynamic-update-slice_fusion.4
  221.3 2.1 constant_dynamic-update-slice_fusion.3
  223.4 1.0 constant_dynamic-update-slice_fusion.2
  224.4 1.0 constant_dynamic-update-slice_fusion.1
  225.3 1.0 constant_dynamic-update-slice_fusion
  226.3 4.7 %constant_dynamic-slice_fusion.5 = bf16[16,2,12,4096]{3,1,2,0:T(2,128)(2,1)} fusion(bf16[32,2,12,4096]{3,1,2,0:T(2,128)(2,1)S(1)} %constant_dynamic-update-slice_fusion, s32[]{:T(128)S(6)} %select_n.58), kind=kLoop, calls=%fused_computation.38 | loop fusion | bytes 6291460 | tf_op jit(solution)/shard_map/jit(_roll_dynamic)/dynamic_slice | solution.py:38
  231.0 4.7 %all-to-all-start.1 = ((bf16[16,2,12,4096]{3,1,2,0:T(2,128)(2,1)}), bf16[16,2,12,4096]{3,1,2,0:T(2,128)(2,1)}, u32[]{:S(2)}, u32[]{:S(2)}) async-start(bf16[16,2,12,4096]{3,1,2,0:T(2,128)(2,1)} %constant_dynamic-slice_fusion.5), calls=%async_computation.1 | async-start | bytes 6291456 | tf_op jit(solution)/shard_map/all_to_all | solution.py:41
  235.8 37.6 %all-to-all-done.1 = bf16[16,2,12,4096]{3,1,2,0:T(2,128)(2,1)} async-done(((bf16[16,2,12,4096]{3,1,2,0:T(2,128)(2,1)}), bf16[16,2,12,4096]{3,1,2,0:T(2,128)(2,1)}, u32[]{:S(2)}, u32[]{:S(2)}) %all-to-all-start.1) | async-done | bytes 3145760 | tf_op jit(solution)/shard_map/all_to_all | solution.py:41
  273.4 5.1 %copy.21 = bf16[8,2,2,12,4096]{4,1,3,2,0:T(2,128)(2,1)S(1)} copy(bf16[8,2,2,12,4096]{4,2,3,1,0:T(2,128)(2,1)} %bitcast.12) | data formatting | bytes 6291456 | tf_op jit(solution)/shard_map/all_to_all | solution.py:41
  279.2 1.0 reshape.85
  280.2 1.1 fusion.5
  281.6 2.7 fusion.3
  284.3 3.6 %copy.25 = f32[4,2,12,64,64]{4,3,1,2,0:T(8,128)} copy(f32[4,2,12,64,64]{3,4,0,1,2:T(8,128)} %fusion.3) | data formatting | bytes 3145728 | tf_op jit(solution)/shard_map/mul | solution.py:56
  287.9 4.2 %reshape.71 = f32[4,2,12,4096]{3,1,2,0:T(2,128)} reshape(f32[4,2,12,64,64]{4,3,1,2,0:T(8,128)} %copy.25) | data formatting | bytes 3145728 | tf_op jit(solution)/shard_map/reshape | solution.py:57
  (24 shorter events, 3.2 us)
Async XLA Ops:
  6.5 3.7 %copy-start = (bf16[4,2,47,4096]{3,1,2,0:T(2,128)(2,1)S(1)}, bf16[4,2,47,4096]{3,1,2,0:T(2,128)(2,1)}, u32[]{:S(2)}) copy-start(bf16[4,2,47,4096]{3,1,2,0:T(2,128)(2,1)} %param.5) | copy-start | bytes 9240580
  6.5 107.5 %all-gather.2.cloned.1.call-start = ((), (), s32[]{:S(2)}) async-start(), calls=%async_computation.2 | async-start | bytes 7077888 | tf_op jit(solution)/shard_map/all_gather | solution.py:24
  25.4 6.4 %copy-start.4 = (s32[4]{0:T(128)S(1)}, s32[4]{0:T(128)}, u32[]{:S(2)}) copy-start(s32[4]{0:T(128)} %param.7) | copy-start | bytes 52
  25.4 77.5 %all-to-all-start = ((bf16[4,2,4,12,4096]{4,1,3,0,2:T(2,128)(2,1)}), bf16[4,2,4,12,4096]{4,1,3,0,2:T(2,128)(2,1)}, u32[]{:S(2)}, u32[]{:S(2)}) async-start(bf16[4,2,4,12,4096]{4,1,3,0,2:T(2,128)(2,1)} %broadcast_select_fusion), calls=%async_computation | async-start | bytes 6291456 | tf_op jit(solution)/shard_map/all_to_all | solution.py:22
  152.4 1.2 copy-start.2
  158.2 20.3 %collective-permute-start = (bf16[4,2,12,4096]{3,1,2,0:T(2,128)(2,1)S(1)}, bf16[4,2,12,4096]{3,1,2,0:T(2,128)(2,1)S(1)}, u32[]{:S(2)}, u32[]{:S(2)}) collective-permute-start(bf16[4,2,12,4096]{3,1,2,0:T(2,128)(2,1)S(1)} %reshape.69), channel_id=1, source_target_pairs={{0,8},{8,16},{16,24},{24,0},{1,9},{9,17},{17,25},{25,1},{2,10},{10... | collective-permute-start | bytes 2359304 | tf_op jit(solution)/shard_map/ppermute | solution.py:37
  178.5 19.4 %collective-permute-start.1 = (bf16[4,2,12,4096]{3,1,2,0:T(2,128)(2,1)S(1)}, bf16[4,2,12,4096]{3,1,2,0:T(2,128)(2,1)S(1)}, u32[]{:S(2)}, u32[]{:S(2)}) collective-permute-start(bf16[4,2,12,4096]{3,1,2,0:T(2,128)(2,1)S(1)} %collective-permute-done), channel_id=1, source_target_pairs={{0,8},{8,16},{16,24},{24,0},{1,9},{9,17},{17,25},{25,1},{2,10},{10... | collective-permute-start | bytes 2359304 | tf_op jit(solution)/shard_map/ppermute | solution.py:37
  197.9 18.6 %collective-permute-start.2 = (bf16[4,2,12,4096]{3,1,2,0:T(2,128)(2,1)S(1)}, bf16[4,2,12,4096]{3,1,2,0:T(2,128)(2,1)}, u32[]{:S(2)}, u32[]{:S(2)}) collective-permute-start(bf16[4,2,12,4096]{3,1,2,0:T(2,128)(2,1)S(1)} %collective-permute-done.1), channel_id=1, source_target_pairs={{0,8},{8,16},{16,24},{24,0},{1,9},{9,17},{17,25},{25,1},{2,10},{10... | collective-permute-start | bytes 2359304 | tf_op jit(solution)/shard_map/ppermute | solution.py:37
  231.0 42.3 %all-to-all-start.1 = ((bf16[16,2,12,4096]{3,1,2,0:T(2,128)(2,1)}), bf16[16,2,12,4096]{3,1,2,0:T(2,128)(2,1)}, u32[]{:S(2)}, u32[]{:S(2)}) async-start(bf16[16,2,12,4096]{3,1,2,0:T(2,128)(2,1)} %constant_dynamic-slice_fusion.5), calls=%async_computation.1 | async-start | bytes 6291456 | tf_op jit(solution)/shard_map/all_to_all | solution.py:41
  280.2 1.4 copy-start.3
  281.6 10.4 %copy-start.1 = (bf16[4,2,47,4096]{3,1,2,0:T(2,128)(2,1)S(1)}, bf16[4,2,47,4096]{3,1,2,0:T(2,128)(2,1)}, u32[]{:S(2)}) copy-start(bf16[4,2,47,4096]{3,1,2,0:T(2,128)(2,1)} %param.5) | copy-start | bytes 9240580
Sparse Core Ops, SparseCore 0:
  9.5 48.1 all-gather.1
